TPU v7x, 128 devices: a whole 4x4x4 slice. The times are simulated.
128 devices in a mesh: dp: 16 (over z, y_hi, core), tensor: 8 (over x, y_lo).
Axes of the slice: x: 4, y: 4 (y_hi: 2, y_lo: 2; y = y_hi * 2 + y_lo), z: 4, core: 2. Of those that a mesh axis runs over, the one named last changes fastest.
Arguments:
- train_states: bfloat16 [4096, 8192], P('dp'), may hold values from -6 to 6
- qkv_cotangent: bfloat16 [4096, 6144], P('dp', 'tensor'), may hold values from -0.09375 to 0.09375
- w_master: float32 [8192, 6144], P('dp', 'tensor'), may hold values from -1.1048543 to 1.1048543
- moment_one: float32 [8192, 6144], P('dp', 'tensor'), may hold values from -1.8 to 1.8
- moment_two: float32 [8192, 6144], P('dp', 'tensor'), may hold values from 0.02 to 2
- prompt_states: bfloat16 [8192, 8192], P('dp'), may hold values from -45 to 45
- norm_gain: float32 [8192], replicated, may hold values from 0.1 to 1.9
- w_out: bfloat16 [4096, 8192], P('tensor'), may hold values from -0.09375 to 0.09375
Outputs:
- update_dir: float32 [8192, 6144], P('dp', 'tensor')
- prefill_out: bfloat16 [8192, 8192], P(('dp', 'tensor'))
All inputs are finite; a program needn't handle non-finite values.
Results may differ from a plain program's by a relative error of at most 0.02.
Values may be sent and summed in bfloat16 or wider, within the bound.
A program may use at most 128 MiB of HBM per device.

v0:
```python
import jax
import jax.numpy as jnp
from jax import lax
from jax.sharding import PartitionSpec as P

HD = 128
beta_one = 0.9
beta_two = 0.95
bias_one = 1.0 - 0.9**8
bias_two = 1.0 - 0.95**8
learn_rate = 0.002
adam_eps = 1e-08
norm_eps = 1e-05
rope_base = 500000.0


def rope_tables(length, head_size):
    half_width = head_size // 2
    exponent = jnp.arange(half_width, dtype=jnp.float32) * (2.0 / head_size)
    inverse = jnp.power(jnp.float32(rope_base), -exponent)
    position = jnp.arange(length, dtype=jnp.float32)
    angles = position[:, None] * inverse[None, :]
    cosine_table = jnp.concatenate([jnp.cos(angles), jnp.cos(angles)], axis=1)
    sine_table = jnp.concatenate([jnp.sin(angles), jnp.sin(angles)], axis=1)
    return (cosine_table, sine_table)


def rotate(head_block, cosine_table, sine_table):
    half_width = head_block.shape[-1] // 2
    turned = jnp.concatenate([-head_block[..., half_width:], head_block[..., :half_width]], axis=-1)
    return head_block * cosine_table + turned * sine_table


def body(
    train_states, qkv_cotangent, w_master, moment_one, moment_two, prompt_states, norm_gain, w_out
):
    slice_width = w_master.shape[1]
    gradient = lax.psum_scatter(
        lax.dot_general(
            train_states,
            qkv_cotangent,
            (((0,), (0,)), ((), ())),
            preferred_element_type=jnp.float32,
        ).astype(jnp.bfloat16),
        "dp",
        scatter_dimension=0,
        tiled=True,
    ).astype(jnp.float32)
    moment_new = beta_one * moment_one + (1.0 - beta_one) * gradient
    second_new = beta_two * moment_two + (1.0 - beta_two) * gradient * gradient
    update_dir = moment_new / bias_one / (jnp.sqrt(second_new / bias_two) + adam_eps)
    owned_weight = (w_master - learn_rate * update_dir).astype(jnp.bfloat16)
    length = prompt_states.shape[0]
    widened = prompt_states.astype(jnp.float32)
    mean_square = jnp.mean(widened * widened, axis=1, keepdims=True)
    normed = (widened * lax.rsqrt(mean_square + norm_eps) * norm_gain).astype(jnp.bfloat16)
    projected = jnp.dot(
        normed,
        lax.all_gather(owned_weight, "dp", axis=0, tiled=True),
        preferred_element_type=jnp.float32,
    )
    query_width = slice_width - 2 * HD
    head_count = query_width // HD
    score_scale = HD ** (-0.5)
    cosine_table, sine_table = rope_tables(length, HD)
    queries = projected[:, :query_width].reshape(length, head_count, HD)
    queries = (
        rotate(queries, cosine_table[:, None, :], sine_table[:, None, :]) * score_scale
    ).astype(jnp.bfloat16)
    key_rows = rotate(
        projected[:, query_width : query_width + HD], cosine_table, sine_table
    ).astype(jnp.bfloat16)
    value_rows = projected[:, query_width + HD :].astype(jnp.bfloat16)
    scores = jnp.einsum("qhd,kd->hqk", queries, key_rows, preferred_element_type=jnp.float32)
    causal = jnp.arange(length)[:, None] >= jnp.arange(length)[None, :]
    scores = jnp.where(causal[None], scores, -jnp.inf)
    attend_weights = jax.nn.softmax(scores, axis=-1).astype(jnp.bfloat16)
    attended = jnp.einsum(
        "hqk,kd->qhd", attend_weights, value_rows, preferred_element_type=jnp.float32
    ).astype(jnp.bfloat16)
    attended = attended.reshape(length, query_width)
    summed = lax.psum_scatter(
        jnp.dot(attended, w_out, preferred_element_type=jnp.float32).astype(jnp.bfloat16),
        "tensor",
        scatter_dimension=0,
        tiled=True,
    )
    return (update_dir, summed)


def solution(mesh):
    placed = (
        P("dp", None),
        P("dp", "tensor"),
        P("dp", "tensor"),
        P("dp", "tensor"),
        P("dp", "tensor"),
        P("dp", None),
        P(),
        P("tensor", None),
    )
    return jax.shard_map(
        body,
        mesh=mesh,
        in_specs=placed,
        out_specs=(P("dp", "tensor"), P(("dp", "tensor"), None)),
        check_vma=False,
    )
```

profile of v0, /device:TPU:1, one launch (start us, length us, event | category | flops | bytes accessed | tf_op | source)
XLA Modules:
  0.0 435.9 jit_solution(55790417744570518)
XLA Ops:
  7.2 0.0 reduce-scatter.3.cloned.1.call-start
  7.2 0.9 copy-done
  8.2 10.2 %convolution_convert_fusion = bf16[8192,768]{1,0:T(8,128)(2,1)} fusion(bf16[256,8192]{1,0:T(8,128)(2,1)} %param.8, bf16[256,768]{1,0:T(8,128)(2,1)S(1)} %copy-done), kind=kOutput, calls=%fused_computation.6 | convolution fusion | flops 3227516928 | bytes 17170432 | tf_op jit(solution)/shard_map/dot_general | solution.py:39
  18.4 0.0 reduce-scatter.3.cloned.1.call-update
  18.4 0.0 all-gather.2.cloned.1.call-start
  18.5 125.2 %reduce-scatter.3.cloned.1.call-done = bf16[512,768]{1,0:T(8,128)(2,1)} async-done(((bf16[8192,768]{1,0:T(8,128)(2,1)}), bf16[512,768]{1,0:T(8,128)(2,1)}) %reduce-scatter.3.cloned.1.call-update) | async-done | bytes 786448 | tf_op jit(solution)/shard_map/reduce_scatter | solution.py:38
  143.7 4.2 subtract_convert_fusion
  147.9 0.0 all-gather.2.cloned.1.call-update
  147.9 0.2 reduce-scatter.5.cloned.1.call-start
  148.2 0.1 iota_compare_fusion
  148.3 1.0 fusion.31
  149.3 0.2 pad_maximum_fusion
  149.5 5.1 %fusion.1 = f32[512]{0:T(512)S(1)} fusion(bf16[512,8192]{1,0:T(8,128)(2,1)} %param.13), kind=kLoop, calls=%fused_computation.3 | loop fusion | flops 12582400 | bytes 8390656 | tf_op jit(solution)/shard_map/reduce_sum | solution.py:55
  154.6 83.7 %all-gather.2.cloned.1.call-done = bf16[8192,768]{1,0:T(8,128)(2,1)} async-done(((bf16[512,768]{1,0:T(8,128)(2,1)}), bf16[8192,768]{1,0:T(8,128)(2,1)}) %all-gather.2.cloned.1.call-update) | async-done | bytes 12582928 | tf_op jit(solution)/shard_map/all_gather | solution.py:59
  238.3 12.0 %fusion.4 = f32[512,768]{1,0:T(8,128)S(1)} fusion(bf16[8192,768]{1,0:T(8,128)(2,1)} %all-gather.2.cloned.1.call-done, bf16[512,8192]{1,0:T(8,128)(2,1)} %param.13, f32[8192]{0:T(1024)S(1)} %copy-done.4, f32[512]{0:T(512)S(1)} %add_rsqrt_fusion), kind=kOutput, calls=%fused_computation.8 | convolution fusion | flops 6459228160 | bytes 22579200 | tf_op jit(solution)/shard_map/dot_general | solution.py:57
  250.3 0.1 copy_bitcast_fusion
  250.4 0.1 slice_negate_fusion.1
  250.5 0.3 slice_negate_fusion
  250.9 0.9 fusion.23
  251.8 1.9 fusion.40
  253.7 0.5 fusion.19
  254.2 1.8 slice-done.1
  256.0 6.9 %convolution_convert_fusion.1 = bf16[512,8192]{1,0:T(8,128)(2,1)} fusion(bf16[512,512]{0,1:T(8,128)(2,1)S(1)} %bitcast.37, bf16[512,8192]{1,0:T(8,128)(2,1)S(1)} %bitcast.36), kind=kOutput, calls=%fused_computation.7 | convolution fusion | flops 4299161600 | bytes 17301504 | tf_op jit(solution)/shard_map/dot_general | solution.py:83
  262.9 166.5 %reduce-scatter.5.cloned.1.call-done = bf16[64,8192]{1,0:T(8,128)(2,1)} async-done(((bf16[512,8192]{1,0:T(8,128)(2,1)}), bf16[64,8192]{1,0:T(8,128)(2,1)}) %reduce-scatter.5.cloned.1.call-update) | async-done | bytes 1048592 | tf_op jit(solution)/shard_map/reduce_scatter | solution.py:82
  (16 shorter events, 0.1 us)
Async XLA Ops:
  7.2 1.0 copy-start
  7.2 136.5 %reduce-scatter.3.cloned.1.call-start = ((), (), s32[]{:S(2)}) async-start(), calls=%async_computation.2 | async-start | bytes 13369344 | tf_op jit(solution)/shard_map/reduce_scatter | solution.py:38
  18.4 125.3 %copy-start.2 = (f32[512,768]{1,0:T(8,128)S(1)}, f32[512,768]{1,0:T(8,128)}, u32[]{:S(2)}) copy-start(f32[512,768]{1,0:T(8,128)} %param.10) | copy-start | bytes 4718596
  18.4 125.3 %copy-start.3 = (f32[512,768]{1,0:T(8,128)S(1)}, f32[512,768]{1,0:T(8,128)}, u32[]{:S(2)}) copy-start(f32[512,768]{1,0:T(8,128)} %param.12) | copy-start | bytes 4718596
  18.4 219.8 %all-gather.2.cloned.1.call-start = ((), (), s32[]{:S(2)}) async-start(), calls=%async_computation.3 | async-start | bytes 13369344 | tf_op jit(solution)/shard_map/all_gather | solution.py:59
  147.9 281.5 %reduce-scatter.5.cloned.1.call-start = ((), (), s32[]{:S(2)}) async-start(), calls=%async_computation.4 | async-start | bytes 9437184 | tf_op jit(solution)/shard_map/reduce_scatter | solution.py:82
  149.5 88.8 %copy-start.4 = (f32[8192]{0:T(1024)S(1)}, f32[8192]{0:T(1024)}, u32[]{:S(2)}) copy-start(f32[8192]{0:T(1024)} %param.14) | copy-start | bytes 98308
  251.8 2.4 slice-start
  253.7 2.3 slice-start.1
  262.8 166.6 %copy-start.1 = (bf16[256,768]{1,0:T(8,128)(2,1)S(1)}, bf16[256,768]{1,0:T(8,128)(2,1)}, u32[]{:S(2)}) copy-start(bf16[256,768]{1,0:T(8,128)(2,1)} %param.9) | copy-start | bytes 1179652
Sparse Core Ops, SparseCore 0:
  18.6 125.0 reduce-scatter.2
  148.1 90.1 all-gather.1
  263.0 166.3 reduce-scatter.4
where the time goes:
time: 436 us
  waiting for transfers between devices  375 us (86%)
  matrix products  30.5 us (7%)
  between operations  13.9 us (3%)
  other arithmetic  13 us (3%)
    reduce_scatter x1, waiting for transfers between devices, body(): lax.psum_scatter(jnp.dot(attended, w_out, preferred_element_type=jnp.floa...  167 us
    reduce_scatter x1, waiting for transfers between devices, body(): lax.psum_scatter(lax.dot_general(train_states, qkv_cotangent, (((0,), (0,...  125 us
    all_gather x1, waiting for transfers between devices, body(): lax.all_gather(owned_weight, 'dp', axis=0, tiled=True)  83.7 us
    dot_general x1, matrix products, body(): jnp.dot(normed, lax.all_gather(owned_weight, 'dp', axis=0, tiled=True), p...  12 us
    dot_general x1, matrix products, body(): lax.dot_general(train_states, qkv_cotangent, (((0,), (0,)), ((), ())), pr...  10.2 us
  transfers between devices with their start and end apart: 3, of which 3 were waited for; matrix products, arithmetic and copies ran while one was open for 1% of the time, Pallas kernels for 0%

commit v1 on v0

--- a/solution.py
+++ b/solution.py
@@ -2,6 +2,7 @@
 import jax.numpy as jnp
 from jax import lax
 from jax.sharding import PartitionSpec as P
+from jax.lax import all_to_all, psum
 
 HD = 128
 beta_one = 0.9
@@ -12,6 +13,15 @@
 adam_eps = 1e-08
 norm_eps = 1e-05
 rope_base = 500000.0
+create_widths = lambda values, axis_tag: jnp.concatenate(
+    all_to_all(
+        jnp.stack([values for _ in range(psum(1, axis_name=axis_tag))]),
+        split_axis=0,
+        axis_name=axis_tag,
+        concat_axis=0,
+    ),
+    axis=0,
+)
 
 
 def rope_tables(length, head_size):
@@ -55,9 +65,7 @@
     mean_square = jnp.mean(widened * widened, axis=1, keepdims=True)
     normed = (widened * lax.rsqrt(mean_square + norm_eps) * norm_gain).astype(jnp.bfloat16)
     projected = jnp.dot(
-        normed,
-        lax.all_gather(owned_weight, "dp", axis=0, tiled=True),
-        preferred_element_type=jnp.float32,
+        normed, create_widths(owned_weight, "dp"), preferred_element_type=jnp.float32
     )
     query_width = slice_width - 2 * HD
     head_count = query_width // HD

time: 436 us -> 500 us (1.15)
  waiting for transfers between devices: 375 us -> 427 us
  starting transfers between devices: 0.3 us -> 6.21 us
  local copies, waits for them, and re-layouts: 2.8 us -> 8.51 us
    all_to_all x0 -> x1, waiting for transfers between devices: none -> 134 us  [all_to_all(jnp.stack([values for _ in range(psum(1, axis_name=axis_tag))]...]
    all_gather x1 -> x0, waiting for transfers between devices: 83.7 us -> none  [body(): lax.all_gather(owned_weight, 'dp', axis=0, tiled=True)]
    all_to_all x0 -> x1, starting transfers between devices: none -> 5.95 us  [all_to_all(jnp.stack([values for _ in range(psum(1, axis_name=axis_tag))]...]
    another operation x0 -> x1, local copies, waits for them, and re-layouts: none -> 5.71 us  [jnp.stack([values for _ in range(psum(1, axis_name=axis_tag))])]
where the time goes in v1:
time: 500 us; the launch traced here: 499 us
  waiting for transfers between devices  427 us (85%)
  matrix products  30.7 us (6%)
  between operations  14.2 us (3%)
  other arithmetic  13.2 us (3%)
  local copies, waits for them, and re-layouts  8.51 us (2%)
  starting transfers between devices  6.21 us (1%)
    reduce_scatter x1, waiting for transfers between devices, body(): lax.psum_scatter(jnp.dot(attended, w_out, preferred_element_type=jnp.floa...  167 us
    all_to_all x1, waiting for transfers between devices, all_to_all(jnp.stack([values for _ in range(psum(1, axis_name=axis_tag))]...  134 us
    reduce_scatter x1, waiting for transfers between devices, body(): lax.psum_scatter(lax.dot_general(train_states, qkv_cotangent, (((0,), (0,...  125 us
    dot_general x1, matrix products, body(): jnp.dot(normed, create_widths(owned_weight, 'dp'), preferred_element_type...  12 us
    dot_general x1, matrix products, body(): lax.dot_general(train_states, qkv_cotangent, (((0,), (0,)), ((), ())), pr...  10.2 us
  transfers between devices with their start and end apart: 3, of which 3 were waited for; matrix products, arithmetic and copies ran while one was open for 1% of the time, Pallas kernels for 0%

profile of v1, /device:TPU:1, one launch (start us, length us, event | category | flops | bytes accessed | tf_op | source)
XLA Modules:
  0.0 499.5 jit_solution(2786637096994930954)
XLA Ops:
  7.2 0.0 reduce-scatter.3.cloned.1.call-start
  7.2 0.9 copy-done
  8.2 10.2 %convolution_convert_fusion = bf16[8192,768]{1,0:T(8,128)(2,1)} fusion(bf16[256,8192]{1,0:T(8,128)(2,1)} %param.8, bf16[256,768]{1,0:T(8,128)(2,1)S(1)} %copy-done), kind=kOutput, calls=%fused_computation.6 | convolution fusion | flops 3227516928 | bytes 17170432 | tf_op jit(solution)/shard_map/dot_general | solution.py:49
  18.4 0.0 reduce-scatter.3.cloned.1.call-update
  18.4 125.2 %reduce-scatter.3.cloned.1.call-done = bf16[512,768]{1,0:T(8,128)(2,1)} async-done(((bf16[8192,768]{1,0:T(8,128)(2,1)}), bf16[512,768]{1,0:T(8,128)(2,1)}) %reduce-scatter.3.cloned.1.call-update) | async-done | bytes 786448 | tf_op jit(solution)/shard_map/reduce_scatter | solution.py:48
  143.7 4.5 subtract_convert_fusion
  148.1 5.7 %stack.2 = bf16[16,512,768]{2,1,0:T(8,128)(2,1)} broadcast(bf16[512,768]{1,0:T(8,128)(2,1)S(1)} %get-tuple-element.2), dimensions={1,2} | broadcast | bytes 13369344 | tf_op jit(solution)/shard_map/stack | solution.py:18
  153.8 6.0 %all-to-all-start = ((bf16[16,512,768]{2,1,0:T(8,128)(2,1)}), bf16[16,512,768]{2,1,0:T(8,128)(2,1)}, u32[]{:S(2)}, u32[]{:S(2)}) async-start(bf16[16,512,768]{2,1,0:T(8,128)(2,1)} %stack.2), calls=%async_computation.1 | async-start | bytes 25165824 | tf_op jit(solution)/shard_map/all_to_all | solution.py:17
  159.8 0.2 reduce-scatter.5.cloned.1.call-start
  160.0 0.1 iota_compare_fusion
  160.1 1.0 fusion.31
  161.1 0.2 pad_maximum_fusion
  161.3 5.1 %fusion.1 = f32[512]{0:T(512)S(1)} fusion(bf16[512,8192]{1,0:T(8,128)(2,1)} %param.13), kind=kLoop, calls=%fused_computation.3 | loop fusion | flops 12582400 | bytes 8390656 | tf_op jit(solution)/shard_map/reduce_sum | solution.py:65
  166.4 134.4 %all-to-all-done = bf16[16,512,768]{2,1,0:T(8,128)(2,1)} async-done(((bf16[16,512,768]{2,1,0:T(8,128)(2,1)}), bf16[16,512,768]{2,1,0:T(8,128)(2,1)}, u32[]{:S(2)}, u32[]{:S(2)}) %all-to-all-start) | async-done | bytes 12582944 | tf_op jit(solution)/shard_map/all_to_all | solution.py:17
  300.9 12.0 %fusion.4 = f32[512,768]{1,0:T(8,128)S(1)} fusion(bf16[8192,768]{1,0:T(8,128)(2,1)} %bitcast, bf16[512,8192]{1,0:T(8,128)(2,1)} %param.13, f32[8192]{0:T(1024)S(1)} %copy-done.3, f32[512]{0:T(512)S(1)} %add_rsqrt_fusion), kind=kOutput, calls=%fused_computation.8 | convolution fusion | flops 6459228160 | bytes 22579200 | tf_op jit(solution)/shard_map/dot_general | solution.py:67
  312.9 0.1 copy_bitcast_fusion
  313.0 0.1 slice_negate_fusion.1
  313.1 0.3 slice_negate_fusion
  313.5 0.9 fusion.23
  314.4 1.9 fusion.40
  316.3 0.5 fusion.19
  316.8 1.8 slice-done.1
  318.6 7.0 %convolution_convert_fusion.1 = bf16[512,8192]{1,0:T(8,128)(2,1)} fusion(bf16[512,512]{0,1:T(8,128)(2,1)S(1)} %bitcast.38, bf16[512,8192]{1,0:T(8,128)(2,1)S(1)} %bitcast.37), kind=kOutput, calls=%fused_computation.7 | convolution fusion | flops 4299161600 | bytes 17301504 | tf_op jit(solution)/shard_map/dot_general | solution.py:91
  325.6 167.0 %reduce-scatter.5.cloned.1.call-done = bf16[64,8192]{1,0:T(8,128)(2,1)} async-done(((bf16[512,8192]{1,0:T(8,128)(2,1)}), bf16[64,8192]{1,0:T(8,128)(2,1)}) %reduce-scatter.5.cloned.1.call-update) | async-done | bytes 1048592 | tf_op jit(solution)/shard_map/reduce_scatter | solution.py:90
  (14 shorter events, 0.1 us)
Async XLA Ops:
  7.2 1.0 copy-start
  7.2 136.5 %reduce-scatter.3.cloned.1.call-start = ((), (), s32[]{:S(2)}) async-start(), calls=%async_computation.3 | async-start | bytes 13369344 | tf_op jit(solution)/shard_map/reduce_scatter | solution.py:48
  18.4 125.3 %copy-start.2 = (f32[512,768]{1,0:T(8,128)S(1)}, f32[512,768]{1,0:T(8,128)}, u32[]{:S(2)}) copy-start(f32[512,768]{1,0:T(8,128)} %param.10) | copy-start | bytes 4718596
  153.8 147.0 %all-to-all-start = ((bf16[16,512,768]{2,1,0:T(8,128)(2,1)}), bf16[16,512,768]{2,1,0:T(8,128)(2,1)}, u32[]{:S(2)}, u32[]{:S(2)}) async-start(bf16[16,512,768]{2,1,0:T(8,128)(2,1)} %stack.2), calls=%async_computation.1 | async-start | bytes 25165824 | tf_op jit(solution)/shard_map/all_to_all | solution.py:17
  159.8 332.8 %reduce-scatter.5.cloned.1.call-start = ((), (), s32[]{:S(2)}) async-start(), calls=%async_computation.4 | async-start | bytes 9437184 | tf_op jit(solution)/shard_map/reduce_scatter | solution.py:90
  161.3 139.5 %copy-start.3 = (f32[8192]{0:T(1024)S(1)}, f32[8192]{0:T(1024)}, u32[]{:S(2)}) copy-start(f32[8192]{0:T(1024)} %param.14) | copy-start | bytes 98308
  314.4 2.4 slice-start
  316.3 2.3 slice-start.1
  325.6 167.1 %copy-start.1 = (bf16[256,768]{1,0:T(8,128)(2,1)S(1)}, bf16[256,768]{1,0:T(8,128)(2,1)}, u32[]{:S(2)}) copy-start(bf16[256,768]{1,0:T(8,128)(2,1)} %param.9) | copy-start | bytes 1179652
Sparse Core Ops, SparseCore 0:
  18.6 125.0 reduce-scatter.2
  325.7 166.8 reduce-scatter.4
